TPU v7x, 256 devices: a whole 4x4x8 slice. The times are simulated.
256 devices in a mesh: member: 8 (over x, core), lat: 8 (over z_hi, y), lon: 4 (over z_lo).
Axes of the slice: x: 4, y: 4, z: 8 (z_hi: 2, z_lo: 4; z = z_hi * 4 + z_lo), core: 2. Of those that a mesh axis runs over, the one named last changes fastest.
Arguments:
- fields: bfloat16 [8, 240, 480, 384], P('member', 'lat', 'lon'), may hold values from -6 to 6
- targets: float32 [73, 240, 480], P(None, 'lat', 'lon'), may hold values from -6 to 6
- filt_re: float32 [8, 240, 384], P('member', 'lon', 'lat'), may hold values from -6 to 6
- filt_im: float32 [8, 240, 384], P('member', 'lon', 'lat'), may hold values from -6 to 6
- w_in: bfloat16 [8, 384, 384], P('member'), may hold values from -0.3125 to 0.3125
- b_in: float32 [8, 384], P('member'), may hold values from -3 to 3
- w_out: bfloat16 [8, 73, 384], P('member'), may hold values from -0.3125 to 0.3125
- b_out: float32 [8, 73], P('member'), may hold values from -6 to 6
Outputs:
- nll: float32 [73, 240, 480], P(None, 'lat', 'lon')
- grad_re: float32 [8, 240, 384], P('member', 'lon', 'lat')
- grad_im: float32 [8, 240, 384], P('member', 'lon', 'lat')
All inputs are finite; a program needn't handle non-finite values.
Results may differ from a plain program's by a relative error of at most 0.02.
Values may be sent and summed in bfloat16 or wider, within the bound.
A program may use at most 128 MiB of HBM per device.

v0:
```python
import jax
import jax.numpy as jnp
from jax import lax
from jax.sharding import PartitionSpec as P

variance_floor = 0.1


def side_by_side(arrays, axis, split_dim, concat_dim, along):
    ends, at = ([], 0)
    for a in arrays[:-1]:
        at += a.shape[along]
        ends.append(at)
    both = jnp.concatenate(arrays, axis=along)
    return tuple(
        jnp.split(
            lax.all_to_all(both, axis, split_axis=split_dim, concat_axis=concat_dim, tiled=True),
            ends,
            axis=along,
        )
    )


def cut_along(shard, dim, length):
    before, after = (shard.shape[:dim], shard.shape[dim + 1 :])
    return jnp.moveaxis(shard.reshape(*before, length, -1, *after), dim, 0)


def laid_out(blocks, dim):
    lengths = list(blocks.shape[1:])
    lengths[dim] *= blocks.shape[0]
    return jnp.moveaxis(blocks, 0, dim).reshape(lengths)


def joined_exchange(shard, axis, axes, splits, concats):
    sizes = [lax.axis_size(a) for a in axes]
    blocks = cut_along(shard, splits[0], sizes[0])
    blocks = jnp.moveaxis(cut_along(blocks, splits[1] + 1, sizes[1]), 0, 1)
    inside = blocks.shape[2:]
    blocks = blocks.reshape(-1, *inside)
    blocks = lax.all_to_all(blocks, axis, split_axis=0, concat_axis=0, tiled=True)
    blocks = laid_out(blocks.reshape(*sizes, *inside), concats[0] + 1)
    return laid_out(blocks, concats[1])


def filled_up(lines, length):
    spare = -lines.shape[0] % length
    if not spare:
        return lines
    return jnp.concatenate([lines, jnp.zeros((spare, *lines.shape[1:]), lines.dtype)])


def sum_by_parts(shard, axis):
    lines = shard.reshape(-1, *shard.shape[1:][-1:])
    padded = filled_up(lines, lax.axis_size(axis))
    own = lax.psum_scatter(padded, axis, scatter_dimension=0, tiled=True)
    whole = lax.all_gather(own, axis, axis=0, tiled=True)
    return whole[: len(lines)].reshape(shard.shape)


def lat_table(rows):
    degree = jnp.arange(rows, dtype=jnp.float32)[:, None]
    column = jnp.arange(rows, dtype=jnp.float32)[None, :]
    scale = jnp.where(degree == 0, jnp.sqrt(1.0 / rows), jnp.sqrt(2.0 / rows))
    return (scale * jnp.cos(jnp.pi * degree * (column + 0.5) / rows)).astype(jnp.bfloat16)


def lon_table(columns):
    half_modes = columns // 2
    place = jnp.arange(columns, dtype=jnp.int32)[:, None]
    order = jnp.arange(half_modes, dtype=jnp.int32)[None, :]
    angle = 2.0 * jnp.pi * (place * order % columns).astype(jnp.float32) / columns
    scale = jnp.where(order == 0, jnp.sqrt(1.0 / columns), jnp.sqrt(2.0 / columns))
    return jnp.concatenate([scale * jnp.cos(angle), -scale * jnp.sin(angle)], axis=1).astype(
        jnp.bfloat16
    )


def mode_mask(degrees, half_modes):
    degree = jnp.arange(degrees, dtype=jnp.int32)
    order = jnp.arange(2 * half_modes, dtype=jnp.int32) % half_modes
    return (degree[:, None] >= order[None, :]).astype(jnp.float32)


def apply_filter(spectrum, weight_re, weight_im, keep_modes):
    half_modes = spectrum.shape[2] // 2
    spec_re = spectrum[:, :, :half_modes]
    spec_im = spectrum[:, :, half_modes:]
    keep_half = keep_modes[None, :, :half_modes, None]
    wre = weight_re[:, :, None, :]
    wim = weight_im[:, :, None, :]
    out_re = keep_half * (wre * spec_re - wim * spec_im)
    out_im = keep_half * (wre * spec_im + wim * spec_re)
    return jnp.concatenate([out_re, out_im], axis=2).astype(jnp.bfloat16)


def filter_grads(spectrum, g_spec, keep_modes):
    half_modes = spectrum.shape[2] // 2
    keep_half = keep_modes[None, :, :half_modes, None]
    spec_re = spectrum[:, :, :half_modes]
    spec_im = spectrum[:, :, half_modes:]
    grad_sre = g_spec[:, :, :half_modes]
    grad_sim = g_spec[:, :, half_modes:]
    grad_wre = jnp.sum(keep_half * (grad_sre * spec_re + grad_sim * spec_im), axis=2)
    grad_wim = jnp.sum(keep_half * (grad_sim * spec_re - grad_sre * spec_im), axis=2)
    return (grad_wre, grad_wim)


def lat_forward(lat_basis, grid_field):
    return jnp.einsum(
        "kj,mjlc->mklc", lat_basis, grid_field, preferred_element_type=jnp.float32
    ).astype(jnp.bfloat16)


def lon_forward(lon_basis, coef):
    return jnp.einsum("mklc,lq->mkqc", coef, lon_basis, preferred_element_type=jnp.float32)


def lon_inverse(lon_basis, filtered):
    return jnp.einsum(
        "mkqc,lq->mklc", filtered, lon_basis, preferred_element_type=jnp.float32
    ).astype(jnp.bfloat16)


def lat_inverse(lat_basis, lon_back):
    return jnp.einsum(
        "kj,mklc->mjlc", lat_basis, lon_back, preferred_element_type=jnp.float32
    ).astype(jnp.bfloat16)


def on_device(fields, targets, filt_re, filt_im, w_in, b_in, w_out, b_out):
    lat_parts = lax.axis_size("lat")
    lon_parts = lax.axis_size("lon")
    rows = fields.shape[1] * lat_parts
    columns = fields.shape[2] * lon_parts
    width = fields.shape[3]
    half_modes = columns // 2
    lat_basis = lat_table(rows)
    lon_basis = lon_table(columns)
    keep_modes = mode_mask(rows, half_modes)
    weight_re, weight_im = side_by_side((filt_re, filt_im), "lon", 2, 1, 0)

    def to_spectral(grid_field):
        whole_grid = joined_exchange(grid_field, ("lat", "lon"), ("lat", "lon"), (3, 3), (1, 2))
        coef = lat_forward(lat_basis, whole_grid)
        return lon_forward(lon_basis, coef)

    spectrum = to_spectral(fields)
    filtered = apply_filter(spectrum, weight_re, weight_im, keep_modes)
    lon_back = lon_inverse(lon_basis, filtered)
    spatial = lat_inverse(lat_basis, lon_back)
    returned = joined_exchange(spatial, ("lat", "lon"), ("lat", "lon"), (1, 2), (3, 3))
    block = width // (lat_parts * lon_parts)
    shaped = returned.reshape(
        returned.shape[0], returned.shape[1], returned.shape[2], lon_parts, lat_parts, block
    )
    spatial = shaped.transpose(0, 1, 2, 4, 3, 5).reshape(
        returned.shape[0], returned.shape[1], returned.shape[2], width
    )
    mixed = (fields.astype(jnp.float32) + spatial.astype(jnp.float32)).astype(jnp.bfloat16)
    preact = (
        jnp.einsum("mjlc,mcd->mjld", mixed, w_in, preferred_element_type=jnp.float32)
        + b_in[:, None, None, :]
    )
    hidden = jax.nn.silu(preact).astype(jnp.bfloat16)
    predicted = (
        jnp.einsum("mjld,mvd->mvjl", hidden, w_out, preferred_element_type=jnp.float32)
        + b_out[:, :, None, None]
    )
    first_sum, second_sum = (
        sum_by_parts(jnp.sum(predicted, axis=0), "member"),
        sum_by_parts(jnp.sum(predicted * predicted, axis=0), "member"),
    )
    members = fields.shape[0] * lax.axis_size("member")
    variables = targets.shape[0]
    ens_mean = first_sum / members
    variance = second_sum / members - ens_mean * ens_mean + variance_floor
    residual = targets - ens_mean
    inv_var = 1.0 / variance
    nll = 0.5 * (jnp.log(variance) + residual * residual * inv_var)
    g_pred = (
        -residual * inv_var / members
        + (inv_var - residual * residual * inv_var * inv_var) * (predicted - ens_mean) / members
    ) / variables
    g_hidden = jnp.einsum(
        "mvjl,mvd->mjld", g_pred, w_out.astype(jnp.float32), precision=lax.Precision.HIGHEST
    )
    sigma = jax.nn.sigmoid(preact)
    g_preact = (g_hidden * sigma * (1.0 + preact * (1.0 - sigma))).astype(jnp.bfloat16)
    g_mixed = jnp.einsum(
        "mjld,mcd->mjlc", g_preact, w_in, preferred_element_type=jnp.float32
    ).astype(jnp.bfloat16)
    g_spec = to_spectral(g_mixed)
    grad_re, grad_im = filter_grads(spectrum, g_spec, keep_modes)
    grad_re, grad_im = side_by_side((grad_re, grad_im), "lon", 1, 2, 0)
    return (nll, grad_re, grad_im)


def solution(mesh):
    placed = (
        P("member", "lat", "lon", None),
        P(None, "lat", "lon"),
        P("member", "lon", "lat"),
        P("member", "lon", "lat"),
        P("member", None, None),
        P("member", None),
        P("member", None, None),
        P("member", None),
    )
    return jax.shard_map(
        on_device,
        mesh=mesh,
        in_specs=placed,
        out_specs=(P(None, "lat", "lon"), P("member", "lon", "lat"), P("member", "lon", "lat")),
        check_vma=False,
    )
```

profile of v0, /device:TPU:8, one launch (start us, length us, event | category | flops | bytes accessed | tf_op | source)
XLA Modules:
  0.0 492.0 jit_solution(11296740642952690661)
XLA Ops:
  8.8 5.9 %all-to-all-start = ((f32[4,1,1440]{2,1,0:T(1,128)}), f32[4,1,1440]{2,1,0:T(1,128)S(1)}, u32[]{:S(2)}, u32[]{:S(2)}) async-start(f32[4,1,1440]{2,1,0:T(1,128)} %reshape.258), calls=%async_computation | async-start | bytes 49152 | tf_op jit(solution)/shard_map/all_to_all | solution.py:17
  14.7 3.7 copy.211
  26.8 9.9 %all-to-all-start.1 = ((bf16[32,1,30,120,12]{3,2,4,1,0:T(8,128)(2,1)}), bf16[32,1,30,120,12]{3,2,4,1,0:T(8,128)(2,1)S(1)}, u32[]{:S(2)}, u32[]{:S(2)}) async-start(bf16[32,1,30,120,12]{3,2,4,1,0:T(8,128)(2,1)} %copy.213), calls=%async_computation.1 | async-start | bytes 6291456 | tf_op jit(solution)/shard_map/all_to_all | solution.py:41
  42.0 67.3 %all-to-all-done.1 = bf16[32,1,30,120,12]{3,2,4,1,0:T(8,128)(2,1)S(1)} async-done(((bf16[32,1,30,120,12]{3,2,4,1,0:T(8,128)(2,1)}), bf16[32,1,30,120,12]{3,2,4,1,0:T(8,128)(2,1)S(1)}, u32[]{:S(2)}, u32[]{:S(2)}) %all-to-all-start.1) | async-done | bytes 2764832 | tf_op jit(solution)/shard_map/all_to_all | solution.py:41
  112.3 3.9 copy.216
  116.2 8.1 %fusion.20 = f32[1,240,480,12]{1,2,3,0:T(8,128)} fusion(bf16[240,480,12]{0,1,2:T(8,128)(2,1)} %bitcast.167, bf16[480,240]{0,1:T(8,128)(2,1)S(1)} %copy-done.6, bf16[480,240]{0,1:T(8,128)(2,1)} %get-tuple-element.49, f32[240]{0:T(256)S(1)} %get-tuple-element.51, f32[240]{0:T(256)S(1)} %iota_multiply_fusion, f32[240]{0:T(256)S(1)} %get-tuple-element.50), kind=kOutput, calls=%fused_computation.29 | convolution fusion | flops 1993190400 | bytes 8758080 | tf_op jit(solution)/shard_map/mklc,lq->mkqc/dot_general | solution.py:116
  124.3 3.7 fusion.39
  128.0 6.0 %convert_bitcast_fusion = bf16[1,240,480,12]{1,2,3,0:T(8,128)(2,1)} fusion(bf16[240,240,12]{0,1,2:T(8,128)(2,1)S(1)} %get-tuple-element.33, bf16[240,240,12]{0,1,2:T(8,128)(2,1)S(1)} %get-tuple-element.32, bf16[480,240]{0,1:T(8,128)(2,1)} %get-tuple-element.48, bf16[480,240]{0,1:T(8,128)(2,1)} %get-tuple-element.49, f32[240]{0:T(256)S(1)} %get-tuple-element.51, ...), kind=kOutput, calls=%fused_computation.20 | convolution fusion | flops 2000102400 | bytes 5993280 | tf_op jit(solution)/shard_map/kj,mklc->mjlc/dot_general | solution.py:126
  137.1 3.6 reshape_transpose_reshape.3
  147.7 7.0 %all-to-all-start.2 = ((bf16[32,1,30,120,12]{3,2,4,1,0:T(8,128)(2,1)}), bf16[32,1,30,120,12]{3,2,4,1,0:T(8,128)(2,1)S(1)}, u32[]{:S(2)}, u32[]{:S(2)}) async-start(bf16[32,1,30,120,12]{3,2,4,1,0:T(8,128)(2,1)} %copy.223), calls=%async_computation.2 | async-start | bytes 6291456 | tf_op jit(solution)/shard_map/all_to_all | solution.py:41
  155.1 71.3 %all-to-all-done.2 = bf16[32,1,30,120,12]{3,2,4,1,0:T(8,128)(2,1)S(1)} async-done(((bf16[32,1,30,120,12]{3,2,4,1,0:T(8,128)(2,1)}), bf16[32,1,30,120,12]{3,2,4,1,0:T(8,128)(2,1)S(1)}, u32[]{:S(2)}, u32[]{:S(2)}) %all-to-all-start.2) | async-done | bytes 2764832 | tf_op jit(solution)/shard_map/all_to_all | solution.py:41
  228.6 7.2 %copy.225 = f32[1,30,120,8,4,12]{2,0,5,4,3,1:T(1,128)} copy(f32[1,30,120,8,4,12]{2,4,5,3,1,0:T(4,128)S(1)} %bitcast.154) | data formatting | bytes 11059200 | tf_op jit(solution)/shard_map/convert_element_type | solution.py:160
  235.8 13.0 %copy.226 = f32[1,30,120,384]{3,2,1,0:T(8,128)} copy(f32[1,30,120,384]{2,0,3,1:T(1,128)} %bitcast.153) | data formatting | bytes 11059200 | tf_op jit(solution)/shard_map/convert_element_type | solution.py:160
  248.8 4.7 fusion.16
  261.2 23.1 %fusion.93 = (f32[288,120]{1,0:T(8,128)S(1)}, f32[288,120]{1,0:T(8,128)S(1)}) fusion(f32[2192,120]{1,0:T(8,128)S(1)} %concatenate.39, f32[2192,120]{1,0:T(8,128)} %concatenate.40), kind=kCustom, calls=%all-reduce-scatter.2 | all-reduce-scatter fusion | flops 552961 | bytes 2381824
  292.0 19.0 %all-gather.7.cloned.1.call-done = f32[8,274,120]{2,1,0:T(8,128)} async-done(((f32[1,274,120]{2,1,0:T(8,128)}), f32[8,274,120]{2,1,0:T(8,128)}) %all-gather.7.cloned.1.call-update) | async-done | bytes 1052176 | tf_op jit(solution)/shard_map/all_gather | solution.py:57
  313.3 25.5 %all-gather.5.cloned.1.call-done = f32[8,274,120]{2,1,0:T(8,128)} async-done(((f32[1,274,120]{2,1,0:T(8,128)}), f32[8,274,120]{2,1,0:T(8,128)}) %all-gather.5.cloned.1.call-update) | async-done | bytes 1052176 | tf_op jit(solution)/shard_map/all_gather | solution.py:57
  351.2 7.2 %fusion.38 = bf16[30,120,384]{2,1,0:T(8,128)(2,1)} fusion(f32[30,120,384]{2,1,0:T(8,128)S(1)} %fusion.41, f32[30,120,384]{2,1,0:T(8,128)} %copy-done.2, f32[384]{0:T(512)S(1)} %reduce.2, bf16[1,384,384]{2,1,0:T(8,128)(2,1)S(1)} %copy-done), kind=kOutput, calls=%fused_computation.33 | convolution fusion | flops 1076889600 | bytes 14120448 | tf_op jit(solution)/shard_map/mjld,mcd->mjlc/dot_general | solution.py:190
  358.5 3.7 copy.229
  369.2 83.2 %all_to_all.45 = bf16[32,1,30,120,12]{3,2,4,1,0:T(8,128)(2,1)S(1)} all-to-all(bf16[32,1,30,120,12]{3,2,4,1,0:T(8,128)(2,1)S(1)} %copy.231), channel_id=1, replica_groups=mesh['member'=8,'lat'=8,'lon'=4] {'lat','lon'}, dimensions={0} | all-to-all | bytes 5529600 | tf_op jit(solution)/shard_map/all_to_all | solution.py:41
  455.3 3.9 copy.234
  459.2 8.1 %fusion.23 = f32[1,240,480,12]{1,2,3,0:T(8,128)} fusion(bf16[240,480,12]{0,1,2:T(8,128)(2,1)} %bitcast.166, bf16[480,240]{0,1:T(8,128)(2,1)S(1)} %copy-done.7, bf16[480,240]{0,1:T(8,128)(2,1)} %get-tuple-element.49, f32[240]{0:T(256)S(1)} %get-tuple-element.51, f32[240]{0:T(256)S(1)} %iota_multiply_fusion, f32[240]{0:T(256)S(1)} %get-tuple-element.50), kind=kOutput, calls=%fused_computation.30 | convolution fusion | flops 1993190400 | bytes 8758080 | tf_op jit(solution)/shard_map/mklc,lq->mkqc/dot_general | solution.py:116
  467.3 5.8 %multiply_reduce_fusion.1 = (f32[240,12]{0,1:T(8,128)S(1)}, f32[240,12]{0,1:T(8,128)S(1)}) fusion(f32[1,240,480,12]{1,2,3,0:T(8,128)} %fusion.23, f32[1,240,480,12]{1,2,3,0:T(8,128)} %fusion.20, f32[240,240]{0,1:T(8,128)S(1)} %copy-done.5), kind=kLoop, calls=%fused_computation.18 | loop fusion | flops 6906240 | bytes 11312640 | tf_op jit(solution)/shard_map/reduce_sum | solution.py:104
  473.6 8.8 %all_to_all.46 = f32[4,1,1440]{2,1,0:T(1,128)S(1)} all-to-all(f32[4,1,1440]{2,1,0:T(1,128)S(1)} %reshape.260), channel_id=1, replica_groups=mesh['member'=8,'lat'=8,'lon'=4] {'lon'}, dimensions={0} | all-to-all | bytes 46080 | tf_op jit(solution)/shard_map/all_to_all | solution.py:17
  (99 shorter events, 73.1 us)
Async XLA Ops:
  7.2 241.7 %copy-start = (bf16[1,384,384]{2,1,0:T(8,128)(2,1)S(1)}, bf16[1,384,384]{2,1,0:T(8,128)(2,1)}, u32[]{:S(2)}) copy-start(bf16[1,384,384]{2,1,0:T(8,128)(2,1)} %param.12) | copy-start | bytes 884740
  8.8 18.1 %all-to-all-start = ((f32[4,1,1440]{2,1,0:T(1,128)}), f32[4,1,1440]{2,1,0:T(1,128)S(1)}, u32[]{:S(2)}, u32[]{:S(2)}) async-start(f32[4,1,1440]{2,1,0:T(1,128)} %reshape.258), calls=%async_computation | async-start | bytes 49152 | tf_op jit(solution)/shard_map/all_to_all | solution.py:17
  26.8 82.5 %all-to-all-start.1 = ((bf16[32,1,30,120,12]{3,2,4,1,0:T(8,128)(2,1)}), bf16[32,1,30,120,12]{3,2,4,1,0:T(8,128)(2,1)S(1)}, u32[]{:S(2)}, u32[]{:S(2)}) async-start(bf16[32,1,30,120,12]{3,2,4,1,0:T(8,128)(2,1)} %copy.213), calls=%async_computation.1 | async-start | bytes 6291456 | tf_op jit(solution)/shard_map/all_to_all | solution.py:41
  112.3 3.9 copy-start.6
  116.2 8.1 %copy-start.4 = (f32[240,240]{0,1:T(8,128)S(1)}, f32[240,240]{0,1:T(8,128)}, u32[]{:S(2)}) copy-start(f32[240,240]{0,1:T(8,128)} %fusion.54) | copy-start | bytes 691204
  147.7 7.3 %copy-start.9 = (f32[1,384]{1,0:T(1,128)S(1)}, f32[1,384]{1,0:T(1,128)}, u32[]{:S(2)}) copy-start(f32[1,384]{1,0:T(1,128)} %param.13) | copy-start | bytes 4612
  147.7 78.6 %all-to-all-start.2 = ((bf16[32,1,30,120,12]{3,2,4,1,0:T(8,128)(2,1)}), bf16[32,1,30,120,12]{3,2,4,1,0:T(8,128)(2,1)S(1)}, u32[]{:S(2)}, u32[]{:S(2)}) async-start(bf16[32,1,30,120,12]{3,2,4,1,0:T(8,128)(2,1)} %copy.223), calls=%async_computation.2 | async-start | bytes 6291456 | tf_op jit(solution)/shard_map/all_to_all | solution.py:41
  154.8 156.2 %all-gather.7.cloned.1.call-start = ((), (), s32[]{:S(2)}) async-start(), calls=%async_computation.6 | async-start | bytes 1290240 | tf_op jit(solution)/shard_map/all_gather | solution.py:57
  235.8 13.0 %copy-start.1 = (bf16[1,30,120,384]{3,2,1,0:T(8,128)(2,1)S(1)}, bf16[1,30,120,384]{3,2,1,0:T(8,128)(2,1)}, u32[]{:S(2)}) copy-start(bf16[1,30,120,384]{3,2,1,0:T(8,128)(2,1)} %param.8) | copy-start | bytes 8294404
  248.8 4.7 copy-start.8
  253.5 2.4 copy-start.2
  253.5 2.4 copy-start.10
  258.5 1.6 copy-start.3
  260.1 25.5 %copy-start.11 = (u32[256]{0:T(256)S(1)}, u32[256]{0:T(256)}, u32[]{:S(2)}) copy-start(u32[256]{0:T(256)} %constant.79) | copy-start | bytes 3076
  284.3 2.6 collective-permute-start.1
  288.1 50.8 %all-gather.5.cloned.1.call-start = ((), (), s32[]{:S(2)}) async-start(), calls=%async_computation.5 | async-start | bytes 1290240 | tf_op jit(solution)/shard_map/all_gather | solution.py:57
  288.1 2.7 collective-permute-start
  455.3 3.9 copy-start.7
  459.2 8.1 %copy-start.5 = (f32[240,240]{0,1:T(8,128)S(1)}, f32[240,240]{0,1:T(8,128)}, u32[]{:S(2)}) copy-start(f32[240,240]{0,1:T(8,128)} %fusion.54) | copy-start | bytes 691204
Sparse Core Ops, SparseCore 0:
  288.2 22.6 all-gather.6
  312.8 26.0 all-gather.4
where the time goes:
time: 499 us; the launch traced here: 492 us
  waiting for transfers between devices  184 us (37%)
  blocking collectives  115 us (23%)
  local copies, waits for them, and re-layouts  88.8 us (18%)
  matrix products  38.7 us (8%)
  starting transfers between devices  26.6 us (5%)
  other arithmetic  23.8 us (5%)
  between operations  15.4 us (3%)
    all_to_all x2, waiting for transfers between devices, joined_exchange(): lax.all_to_all(blocks, axis, split_axis=0, concat_axis=0, tiled=True)  139 us
    all_to_all x1, blocking collectives, joined_exchange(): lax.all_to_all(blocks, axis, split_axis=0, concat_axis=0, tiled=True)  83.2 us
    all_gather x2, waiting for transfers between devices, sum_by_parts(): whole = lax.all_gather(own, axis, axis=0, tiled=True)  44.5 us
    unnamed x1, blocking collectives  23.1 us
    convert_element_type x3, local copies, waits for them, and re-layouts, on_device(): spatial.astype(jnp.float32)  22.5 us
    all_to_all x2, starting transfers between devices, joined_exchange(): lax.all_to_all(blocks, axis, split_axis=0, concat_axis=0, tiled=True)  16.9 us
    dot_general x2, matrix products, lon_forward(): jnp.einsum('mklc,lq->mkqc', coef, lon_basis, preferred_element_type=jnp.f...  16.1 us
    unnamed x38, local copies, waits for them, and re-layouts  11.5 us
  transfers between devices with their start and end apart: 7, of which 5 were waited for; matrix products, arithmetic and copies ran while one was open for 4% of the time, Pallas kernels for 0%

commit v1 on v0

--- a/solution.py
+++ b/solution.py
@@ -54,7 +54,9 @@
     lines = shard.reshape(-1, *shard.shape[1:][-1:])
     padded = filled_up(lines, lax.axis_size(axis))
     own = lax.psum_scatter(padded, axis, scatter_dimension=0, tiled=True)
-    whole = lax.all_gather(own, axis, axis=0, tiled=True)
+    whole = jnp.concatenate(
+        lax.all_to_all(jnp.stack([own] * lax.axis_size(axis)), axis, 0, 0), axis=0
+    )
     return whole[: len(lines)].reshape(shard.shape)
 
 

time: 499 us -> 476 us (0.954)
  waiting for transfers between devices: 184 us -> 166 us
  between operations: 15.4 us -> 1.97 us
  starting transfers between devices: 26.6 us -> 35 us
    all_gather x2 -> x0, waiting for transfers between devices: 44.5 us -> none  [sum_by_parts(): whole = lax.all_gather(own, axis, axis=0, tiled=True)]
    all_to_all x0 -> x2, waiting for transfers between devices: none -> 26 us  [sum_by_parts(): lax.all_to_all(jnp.stack([own] * lax.axis_size(axis)), axis, 0, 0)]
    all_to_all x0 -> x2, starting transfers between devices: none -> 8.22 us  [sum_by_parts(): lax.all_to_all(jnp.stack([own] * lax.axis_size(axis)), axis, 0, 0)]
    unnamed x38 -> x36, local copies, waits for them, and re-layouts: 11.5 us -> 7.58 us
  transfers between devices with their start and end apart: 7 -> 7, of which waited for: 5 -> 5; matrix products, arithmetic and copies ran while one was open for 4% -> 5% of each run, Pallas kernels for 0% -> 0%
where the time goes in v1:
time: 476 us; the launch traced here: 469 us
  waiting for transfers between devices  166 us (35%)
  blocking collectives  111 us (23%)
  local copies, waits for them, and re-layouts  90.4 us (19%)
  matrix products  38.7 us (8%)
  starting transfers between devices  35 us (7%)
  other arithmetic  26.4 us (6%)
    all_to_all x2, waiting for transfers between devices, joined_exchange(): lax.all_to_all(blocks, axis, split_axis=0, concat_axis=0, tiled=True)  139 us
    all_to_all x1, blocking collectives, joined_exchange(): lax.all_to_all(blocks, axis, split_axis=0, concat_axis=0, tiled=True)  79 us
    all_to_all x2, waiting for transfers between devices, sum_by_parts(): lax.all_to_all(jnp.stack([own] * lax.axis_size(axis)), axis, 0, 0)  26 us
    unnamed x1, blocking collectives  23.1 us
    convert_element_type x3, local copies, waits for them, and re-layouts, on_device(): spatial.astype(jnp.float32)  22.5 us
    all_to_all x2, starting transfers between devices, joined_exchange(): lax.all_to_all(blocks, axis, split_axis=0, concat_axis=0, tiled=True)  17.2 us
    dot_general x2, matrix products, lon_forward(): jnp.einsum('mklc,lq->mkqc', coef, lon_basis, preferred_element_type=jnp.f...  16.2 us
    transpose x4, local copies, waits for them, and re-layouts, laid_out(): return jnp.moveaxis(blocks, 0, dim).reshape(lengths)  9.85 us
  transfers between devices with their start and end apart: 7, of which 5 were waited for; matrix products, arithmetic and copies ran while one was open for 5% of the time, Pallas kernels for 0%

profile of v1, /device:TPU:8, one launch (start us, length us, event | category | flops | bytes accessed | tf_op | source)
XLA Modules:
  0.0 468.7 jit_solution(3879830758178472908)
XLA Ops:
  2.2 5.9 %all-to-all-start = ((f32[4,1,1440]{2,1,0:T(1,128)}), f32[4,1,1440]{2,1,0:T(1,128)S(1)}, u32[]{:S(2)}, u32[]{:S(2)}) async-start(f32[4,1,1440]{2,1,0:T(1,128)} %reshape.266), calls=%async_computation | async-start | bytes 49152 | tf_op jit(solution)/shard_map/all_to_all | solution.py:17
  8.1 3.7 copy.211
  20.3 9.9 %all-to-all-start.1 = ((bf16[32,1,30,120,12]{3,2,4,1,0:T(8,128)(2,1)}), bf16[32,1,30,120,12]{3,2,4,1,0:T(8,128)(2,1)S(1)}, u32[]{:S(2)}, u32[]{:S(2)}) async-start(bf16[32,1,30,120,12]{3,2,4,1,0:T(8,128)(2,1)} %copy.213), calls=%async_computation.1 | async-start | bytes 6291456 | tf_op jit(solution)/shard_map/all_to_all | solution.py:41
  35.5 67.3 %all-to-all-done.1 = bf16[32,1,30,120,12]{3,2,4,1,0:T(8,128)(2,1)S(1)} async-done(((bf16[32,1,30,120,12]{3,2,4,1,0:T(8,128)(2,1)}), bf16[32,1,30,120,12]{3,2,4,1,0:T(8,128)(2,1)S(1)}, u32[]{:S(2)}, u32[]{:S(2)}) %all-to-all-start.1) | async-done | bytes 2764832 | tf_op jit(solution)/shard_map/all_to_all | solution.py:41
  105.7 3.9 copy.216
  109.6 8.1 %fusion.20 = f32[1,240,480,12]{1,2,3,0:T(8,128)} fusion(bf16[240,480,12]{0,1,2:T(8,128)(2,1)} %bitcast.163, bf16[480,240]{0,1:T(8,128)(2,1)S(1)} %copy-done.6, bf16[480,240]{0,1:T(8,128)(2,1)} %get-tuple-element.49, f32[240]{0:T(256)S(1)} %get-tuple-element.51, f32[240]{0:T(256)S(1)} %iota_multiply_fusion, f32[240]{0:T(256)S(1)} %get-tuple-element.50), kind=kOutput, calls=%fused_computation.29 | convolution fusion | flops 1993190400 | bytes 8758080 | tf_op jit(solution)/shard_map/mklc,lq->mkqc/dot_general | solution.py:118
  117.8 3.7 fusion.39
  121.5 6.0 %convert_bitcast_fusion = bf16[1,240,480,12]{1,2,3,0:T(8,128)(2,1)} fusion(bf16[240,240,12]{0,1,2:T(8,128)(2,1)S(1)} %get-tuple-element.33, bf16[240,240,12]{0,1,2:T(8,128)(2,1)S(1)} %get-tuple-element.32, bf16[480,240]{0,1:T(8,128)(2,1)} %get-tuple-element.48, bf16[480,240]{0,1:T(8,128)(2,1)} %get-tuple-element.49, f32[240]{0:T(256)S(1)} %get-tuple-element.51, ...), kind=kOutput, calls=%fused_computation.20 | convolution fusion | flops 2000102400 | bytes 5993280 | tf_op jit(solution)/shard_map/kj,mklc->mjlc/dot_general | solution.py:128
  141.3 7.4 %all-to-all-start.2 = ((bf16[32,1,30,120,12]{3,2,4,1,0:T(8,128)(2,1)}), bf16[32,1,30,120,12]{3,2,4,1,0:T(8,128)(2,1)S(1)}, u32[]{:S(2)}, u32[]{:S(2)}) async-start(bf16[32,1,30,120,12]{3,2,4,1,0:T(8,128)(2,1)} %copy.223), calls=%async_computation.2 | async-start | bytes 6291456 | tf_op jit(solution)/shard_map/all_to_all | solution.py:41
  148.7 71.4 %all-to-all-done.2 = bf16[32,1,30,120,12]{3,2,4,1,0:T(8,128)(2,1)S(1)} async-done(((bf16[32,1,30,120,12]{3,2,4,1,0:T(8,128)(2,1)}), bf16[32,1,30,120,12]{3,2,4,1,0:T(8,128)(2,1)S(1)}, u32[]{:S(2)}, u32[]{:S(2)}) %all-to-all-start.2) | async-done | bytes 2764832 | tf_op jit(solution)/shard_map/all_to_all | solution.py:41
  222.3 7.2 %copy.225 = f32[1,30,120,8,4,12]{2,0,5,4,3,1:T(1,128)} copy(f32[1,30,120,8,4,12]{2,4,5,3,1,0:T(4,128)S(1)} %bitcast.150) | data formatting | bytes 11059200 | tf_op jit(solution)/shard_map/convert_element_type | solution.py:162
  229.5 13.0 %copy.226 = f32[1,30,120,384]{3,2,1,0:T(8,128)} copy(f32[1,30,120,384]{2,0,3,1:T(1,128)} %bitcast.149) | data formatting | bytes 11059200 | tf_op jit(solution)/shard_map/convert_element_type | solution.py:162
  242.6 4.7 fusion.16
  254.9 23.1 %fusion.93 = (f32[288,120]{1,0:T(8,128)S(1)}, f32[288,120]{1,0:T(8,128)S(1)}) fusion(f32[2192,120]{1,0:T(8,128)S(1)} %concatenate.39, f32[2192,120]{1,0:T(8,128)} %concatenate.40), kind=kCustom, calls=%all-reduce-scatter.2 | all-reduce-scatter fusion | flops 552961 | bytes 2381824
  289.4 13.8 %all-to-all-done.3 = f32[8,274,120]{2,1,0:T(8,128)S(1)} async-done(((f32[8,274,120]{2,1,0:T(8,128)}), f32[8,274,120]{2,1,0:T(8,128)S(1)}, u32[]{:S(2)}, u32[]{:S(2)}) %all-to-all-start.3) | async-done | bytes 1052192 | tf_op jit(solution)/shard_map/all_to_all | solution.py:58
  304.3 4.7 all-to-all-start.4
  313.8 12.2 %all-to-all-done.4 = f32[8,274,120]{2,1,0:T(8,128)} async-done(((f32[8,274,120]{2,1,0:T(8,128)}), f32[8,274,120]{2,1,0:T(8,128)}, u32[]{:S(2)}, u32[]{:S(2)}) %all-to-all-start.4) | async-done | bytes 1052192 | tf_op jit(solution)/shard_map/all_to_all | solution.py:58
  339.3 7.2 %fusion.38 = bf16[30,120,384]{2,1,0:T(8,128)(2,1)} fusion(f32[30,120,384]{2,1,0:T(8,128)S(1)} %fusion.41, f32[30,120,384]{2,1,0:T(8,128)} %copy-done.2, f32[384]{0:T(512)S(1)} %reduce.2, bf16[1,384,384]{2,1,0:T(8,128)(2,1)S(1)} %copy-done), kind=kOutput, calls=%fused_computation.33 | convolution fusion | flops 1076889600 | bytes 14120448 | tf_op jit(solution)/shard_map/mjld,mcd->mjlc/dot_general | solution.py:192
  346.5 3.7 copy.229
  357.2 79.0 %all_to_all.55 = bf16[32,1,30,120,12]{3,2,4,1,0:T(8,128)(2,1)S(1)} all-to-all(bf16[32,1,30,120,12]{3,2,4,1,0:T(8,128)(2,1)S(1)} %copy.231), channel_id=1, replica_groups=mesh['member'=8,'lat'=8,'lon'=4] {'lat','lon'}, dimensions={0} | all-to-all | bytes 5529600 | tf_op jit(solution)/shard_map/all_to_all | solution.py:41
  439.2 3.9 copy.234
  443.1 8.1 %fusion.23 = f32[1,240,480,12]{1,2,3,0:T(8,128)} fusion(bf16[240,480,12]{0,1,2:T(8,128)(2,1)} %bitcast.162, bf16[480,240]{0,1:T(8,128)(2,1)S(1)} %copy-done.7, bf16[480,240]{0,1:T(8,128)(2,1)} %get-tuple-element.49, f32[240]{0:T(256)S(1)} %get-tuple-element.51, f32[240]{0:T(256)S(1)} %iota_multiply_fusion, f32[240]{0:T(256)S(1)} %get-tuple-element.50), kind=kOutput, calls=%fused_computation.30 | convolution fusion | flops 1993190400 | bytes 8758080 | tf_op jit(solution)/shard_map/mklc,lq->mkqc/dot_general | solution.py:118
  451.2 5.8 %multiply_reduce_fusion.1 = (f32[240,12]{0,1:T(8,128)S(1)}, f32[240,12]{0,1:T(8,128)S(1)}) fusion(f32[1,240,480,12]{1,2,3,0:T(8,128)} %fusion.23, f32[1,240,480,12]{1,2,3,0:T(8,128)} %fusion.20, f32[240,240]{0,1:T(8,128)S(1)} %copy-done.5), kind=kLoop, calls=%fused_computation.18 | loop fusion | flops 6906240 | bytes 11312640 | tf_op jit(solution)/shard_map/reduce_sum | solution.py:106
  457.5 8.5 %all_to_all.56 = f32[4,1,1440]{2,1,0:T(1,128)S(1)} all-to-all(f32[4,1,1440]{2,1,0:T(1,128)S(1)} %reshape.268), channel_id=1, replica_groups=mesh['member'=8,'lat'=8,'lon'=4] {'lon'}, dimensions={0} | all-to-all | bytes 46080 | tf_op jit(solution)/shard_map/all_to_all | solution.py:17
  (99 shorter events, 84.6 us)
Async XLA Ops:
  0.6 241.9 %copy-start = (bf16[1,384,384]{2,1,0:T(8,128)(2,1)S(1)}, bf16[1,384,384]{2,1,0:T(8,128)(2,1)}, u32[]{:S(2)}) copy-start(bf16[1,384,384]{2,1,0:T(8,128)(2,1)} %param.12) | copy-start | bytes 884740
  2.2 18.1 %all-to-all-start = ((f32[4,1,1440]{2,1,0:T(1,128)}), f32[4,1,1440]{2,1,0:T(1,128)S(1)}, u32[]{:S(2)}, u32[]{:S(2)}) async-start(f32[4,1,1440]{2,1,0:T(1,128)} %reshape.266), calls=%async_computation | async-start | bytes 49152 | tf_op jit(solution)/shard_map/all_to_all | solution.py:17
  20.3 82.5 %all-to-all-start.1 = ((bf16[32,1,30,120,12]{3,2,4,1,0:T(8,128)(2,1)}), bf16[32,1,30,120,12]{3,2,4,1,0:T(8,128)(2,1)S(1)}, u32[]{:S(2)}, u32[]{:S(2)}) async-start(bf16[32,1,30,120,12]{3,2,4,1,0:T(8,128)(2,1)} %copy.213), calls=%async_computation.1 | async-start | bytes 6291456 | tf_op jit(solution)/shard_map/all_to_all | solution.py:41
  105.7 3.9 copy-start.6
  109.6 8.1 %copy-start.4 = (f32[240,240]{0,1:T(8,128)S(1)}, f32[240,240]{0,1:T(8,128)}, u32[]{:S(2)}) copy-start(f32[240,240]{0,1:T(8,128)} %fusion.54) | copy-start | bytes 691204
  141.3 7.4 %copy-start.9 = (f32[1,384]{1,0:T(1,128)S(1)}, f32[1,384]{1,0:T(1,128)}, u32[]{:S(2)}) copy-start(f32[1,384]{1,0:T(1,128)} %param.13) | copy-start | bytes 4612
  141.3 78.8 %all-to-all-start.2 = ((bf16[32,1,30,120,12]{3,2,4,1,0:T(8,128)(2,1)}), bf16[32,1,30,120,12]{3,2,4,1,0:T(8,128)(2,1)S(1)}, u32[]{:S(2)}, u32[]{:S(2)}) async-start(bf16[32,1,30,120,12]{3,2,4,1,0:T(8,128)(2,1)} %copy.223), calls=%async_computation.2 | async-start | bytes 6291456 | tf_op jit(solution)/shard_map/all_to_all | solution.py:41
  229.5 13.0 %copy-start.1 = (bf16[1,30,120,384]{3,2,1,0:T(8,128)(2,1)S(1)}, bf16[1,30,120,384]{3,2,1,0:T(8,128)(2,1)}, u32[]{:S(2)}) copy-start(bf16[1,30,120,384]{3,2,1,0:T(8,128)(2,1)} %param.8) | copy-start | bytes 8294404
  242.6 4.7 copy-start.8
  247.2 2.4 copy-start.2
  247.2 2.4 copy-start.10
  252.3 1.6 copy-start.3
  253.8 25.5 %copy-start.11 = (u32[256]{0:T(256)S(1)}, u32[256]{0:T(256)}, u32[]{:S(2)}) copy-start(u32[256]{0:T(256)} %constant.79) | copy-start | bytes 3076
  278.1 2.6 collective-permute-start
  282.2 21.0 %all-to-all-start.3 = ((f32[8,274,120]{2,1,0:T(8,128)}), f32[8,274,120]{2,1,0:T(8,128)S(1)}, u32[]{:S(2)}, u32[]{:S(2)}) async-start(f32[8,274,120]{2,1,0:T(8,128)} %stack.4), calls=%async_computation.3 | async-start | bytes 2293760 | tf_op jit(solution)/shard_map/all_to_all | solution.py:58
  285.8 3.2 collective-permute-start.1
  304.3 21.7 %all-to-all-start.4 = ((f32[8,274,120]{2,1,0:T(8,128)}), f32[8,274,120]{2,1,0:T(8,128)}, u32[]{:S(2)}, u32[]{:S(2)}) async-start(f32[8,274,120]{2,1,0:T(8,128)} %stack.5), calls=%async_computation.4 | async-start | bytes 2293760 | tf_op jit(solution)/shard_map/all_to_all | solution.py:58
  439.2 3.9 copy-start.7
  443.1 8.1 %copy-start.5 = (f32[240,240]{0,1:T(8,128)S(1)}, f32[240,240]{0,1:T(8,128)}, u32[]{:S(2)}) copy-start(f32[240,240]{0,1:T(8,128)} %fusion.54) | copy-start | bytes 691204
